TPU v7x, 32 devices: a whole 2x2x4 slice. The times are simulated.
32 devices in a mesh: gx: 8 (over z, y), gy: 4 (over x, core).
Axes of the slice: x: 2, y: 2, z: 4, core: 2. Of those that a mesh axis runs over, the one named last changes fastest.
Arguments:
- velocity: float32 [3, 64, 32, 128], P(None, 'gx', 'gy'), may hold values from -6 to 6
- surfaces: float32 [8, 6, 64, 32, 128], P(None, None, 'gx', 'gy'), may hold values from -2 to 2
- mean_stress: float32 [64, 32, 128], P('gx', 'gy'), may hold values from -6 to 6
- zone: int32 [64, 32, 128], P('gx', 'gy'), may hold values from 0 to 7
- sponge: int32 [64, 32, 128], P('gx', 'gy'), may hold values from 0 to 3
- moduli: float32 [8, 3], replicated, may hold values from 0.5 to 2
- yields: float32 [8, 8], replicated, may hold values from 0.05 to 1
Outputs:
- new_velocity: float32 [3, 64, 32, 128], P(None, 'gx', 'gy')
- new_stress: float32 [6, 64, 32, 128], P(None, 'gx', 'gy')
All inputs are finite; a program needn't handle non-finite values.
Results may differ from a plain program's by a relative error of at most 0.0001.
Values sent between devices are 32-bit elements; how exact they have to be, the bound alone decides.
A program may use at most 64 MiB of HBM per device.

v0:
```python
import jax
import jax.numpy as jnp
from jax import lax
from jax.sharding import PartitionSpec as P

ITERS = 3


coef_near = 9.0 / 8.0
coef_far = -1.0 / 24.0
time_step = 0.1
sponge_rate = 0.1


def with_halo(block, sides, width):
    for axis, dim in sides:
        count = lax.axis_size(axis)
        forward = [(i, i + 1) for i in range(count - 1)]
        backward = [(target, source) for source, target in forward]
        low = lax.ppermute(
            lax.slice_in_dim(block, block.shape[dim] - width, None, axis=dim), axis, forward
        )
        high = lax.ppermute(lax.slice_in_dim(block, 0, width, axis=dim), axis, backward)
        block = jnp.concatenate([low, block, high], axis=dim)
    return block


def shifted(field, axis_pos, offset):
    lead = field.ndim - 3
    slices = [slice(None)] * lead
    for position in range(3):
        length = field.shape[lead + position]
        if position == axis_pos:
            slices.append(slice(2 + offset, length - 2 + offset))
        else:
            slices.append(slice(2, length - 2))
    return field[tuple(slices)]


def forward(field, axis_pos):
    return coef_near * (shifted(field, axis_pos, 1) - shifted(field, axis_pos, 0)) + coef_far * (
        shifted(field, axis_pos, 2) - shifted(field, axis_pos, -1)
    )


def backward(field, axis_pos):
    return coef_near * (shifted(field, axis_pos, 0) - shifted(field, axis_pos, -1)) + coef_far * (
        shifted(field, axis_pos, 1) - shifted(field, axis_pos, -2)
    )


def lookup(table, zone):
    result = jnp.zeros((table.shape[1],) + zone.shape, table.dtype)
    for index_zone in range(table.shape[0]):
        picked = (zone == index_zone)[None]
        result = result + jnp.where(
            picked, table[index_zone][:, None, None, None], jnp.zeros((), table.dtype)
        )
    return result


def total_stress(surfaces, mean_stress):
    diagonal_mask = jnp.array([1.0, 1.0, 1.0, 0.0, 0.0, 0.0], dtype=jnp.float32)[
        :, None, None, None
    ]
    return jnp.sum(surfaces, axis=0) + diagonal_mask * mean_stress[None]


def advance(velocity, stress_pad, buoyancy, damping):
    accel = jnp.stack(
        [
            forward(stress_pad[0], 0) + backward(stress_pad[3], 1) + backward(stress_pad[4], 2),
            backward(stress_pad[3], 0) + forward(stress_pad[1], 1) + backward(stress_pad[5], 2),
            backward(stress_pad[4], 0) + backward(stress_pad[5], 1) + forward(stress_pad[2], 2),
        ]
    )
    return (velocity + time_step * buoyancy[None] * accel) * damping[None]


def plastic(surfaces, mean_stress, velocity_pad, bulk, shear, limit):
    rate_xx = backward(velocity_pad[0], 0)
    rate_yy = backward(velocity_pad[1], 1)
    rate_zz = backward(velocity_pad[2], 2)
    rate_xy = 0.5 * (forward(velocity_pad[0], 1) + forward(velocity_pad[1], 0))
    rate_xz = 0.5 * (forward(velocity_pad[0], 2) + forward(velocity_pad[2], 0))
    rate_yz = 0.5 * (forward(velocity_pad[1], 2) + forward(velocity_pad[2], 1))
    trace = rate_xx + rate_yy + rate_zz
    mean_stress = mean_stress + time_step * bulk * trace
    third = trace / 3.0
    deviator = jnp.stack(
        [rate_xx - third, rate_yy - third, rate_zz - third, rate_xy, rate_xz, rate_yz]
    )
    trial = surfaces + 2.0 * time_step / 8.0 * shear[None, None] * deviator[None]
    magnitude = jnp.sqrt(
        0.5 * jnp.sum(trial[:, :3] * trial[:, :3], axis=1)
        + jnp.sum(trial[:, 3:] * trial[:, 3:], axis=1)
    )
    factor = limit / jnp.maximum(magnitude, limit)
    surfaces = trial * factor[:, None]
    return (surfaces, mean_stress, total_stress(surfaces, mean_stress))


def pad_depth(field):
    return jnp.pad(field, [(0, 0)] * (field.ndim - 1) + [(2, 2)])


def body(velocity, surfaces, mean_stress, zone, sponge, moduli, yields):
    material = lookup(moduli, zone)
    bulk, shear, buoyancy = (material[0], material[1], material[2])
    limit = lookup(yields, zone)
    damping = 1.0 - sponge_rate * sponge.astype(jnp.float32)
    stress = total_stress(surfaces, mean_stress)
    factors = with_halo(jnp.stack([buoyancy, damping]), (("gx", 1), ("gy", 2)), 2)
    for turn_index in range(ITERS):
        state_wide = with_halo(
            jnp.concatenate([stress, velocity], axis=0), (("gx", 1), ("gy", 2)), 4
        )
        stress_pad = pad_depth(state_wide[:6])
        old_velocity = state_wide[6:, 2:-2, 2:-2, :]
        velocity_wide = advance(old_velocity, stress_pad, factors[0], factors[1])
        velocity = velocity_wide[:, 2:-2, 2:-2, :]
        surfaces, mean_stress, stress = plastic(
            surfaces, mean_stress, pad_depth(velocity_wide), bulk, shear, limit
        )
    return (velocity, stress)


def solution(mesh):
    return jax.shard_map(
        body,
        mesh=mesh,
        in_specs=(
            P(None, "gx", "gy", None),
            P(None, None, "gx", "gy", None),
            P("gx", "gy", None),
            P("gx", "gy", None),
            P("gx", "gy", None),
            P(),
            P(),
        ),
        out_specs=(P(None, "gx", "gy", None), P(None, "gx", "gy", None)),
        check_vma=False,
    )
```

profile of v0, /device:TPU:1, one launch (start us, length us, event | category | flops | bytes accessed | tf_op | source)
XLA Modules:
  0.0 92.4 jit_solution(12092143282259571579)
XLA Ops:
  3.7 4.0 %collective-permute-start.4 = (f32[2,2,8,128]{3,2,1,0:T(8,128)S(1)}, f32[2,2,8,128]{3,2,1,0:T(8,128)S(1)}, u32[]{:S(2)}, u32[]{:S(2)}) collective-permute-start(f32[2,2,8,128]{3,2,1,0:T(8,128)S(1)} %get-tuple-element.78), channel_id=1, source_target_pairs={{0,4},{4,8},{8,12},{12,16},{16,20},{20,24},{24,28},{1,5},{5,9},{9,... | collective-permute-start | bytes 49160 | tf_op jit(solution)/shard_map/ppermute | solution.py:20
  7.7 1.3 %collective-permute-start.5 = (f32[2,2,8,128]{3,2,1,0:T(8,128)S(1)}, f32[2,2,8,128]{3,2,1,0:T(8,128)S(1)}, u32[]{:S(2)}, u32[]{:S(2)}) collective-permute-start(f32[2,2,8,128]{3,2,1,0:T(8,128)S(1)} %get-tuple-element.79), channel_id=1, source_target_pairs={{4,0},{8,4},{12,8},{16,12},{20,16},{24,20},{28,24},{5,1},{9,5},{13... | collective-permute-start | bytes 49160 | tf_op jit(solution)/shard_map/ppermute | solution.py:23
  9.0 1.5 %reduce_sum.90 = f32[6,8,8,128]{3,2,1,0:T(8,128)S(1)} reduce(f32[8,6,8,8,128]{4,3,2,1,0:T(8,128)} %param.12, f32[]{:T(128)} %constant.18.clone.1), dimensions={0}, to_apply=%region_0.1 | reduce | flops 344064 | bytes 1769476 | tf_op jit(solution)/shard_map/reduce_sum | solution.py:66
  10.6 4.0 %collective-permute-start = (f32[9,4,8,128]{3,2,1,0:T(8,128)S(1)}, f32[9,4,8,128]{3,2,1,0:T(8,128)S(1)}, u32[]{:S(2)}, u32[]{:S(2)}) collective-permute-start(f32[9,4,8,128]{3,2,1,0:T(8,128)S(1)} %get-tuple-element.70), channel_id=1, source_target_pairs={{0,4},{4,8},{8,12},{12,16},{16,20},{20,24},{24,28},{1,5},{5,9},{9,... | collective-permute-start | bytes 442376 | tf_op jit(solution)/shard_map/ppermute | solution.py:20
  14.6 1.3 %collective-permute-start.1 = (f32[9,4,8,128]{3,2,1,0:T(8,128)S(1)}, f32[9,4,8,128]{3,2,1,0:T(8,128)S(1)}, u32[]{:S(2)}, u32[]{:S(2)}) collective-permute-start(f32[9,4,8,128]{3,2,1,0:T(8,128)S(1)} %get-tuple-element.71), channel_id=1, source_target_pairs={{4,0},{8,4},{12,8},{16,12},{20,16},{24,20},{28,24},{5,1},{9,5},{13... | collective-permute-start | bytes 442376 | tf_op jit(solution)/shard_map/ppermute | solution.py:23
  16.0 4.5 %collective-permute-start.6 = (f32[2,12,2,128]{3,2,1,0:T(2,128)S(1)}, f32[2,12,2,128]{3,2,1,0:T(2,128)S(1)}, u32[]{:S(2)}, u32[]{:S(2)}) collective-permute-start(f32[2,12,2,128]{3,2,1,0:T(2,128)S(1)} %get-tuple-element.76), channel_id=1, source_target_pairs={{0,1},{1,2},{2,3},{4,5},{5,6},{6,7},{8,9},{9,10},{10,11},{12,13},{... | collective-permute-start | bytes 73736 | tf_op jit(solution)/shard_map/ppermute | solution.py:20
  20.5 1.9 %collective-permute-start.7 = (f32[2,12,2,128]{3,2,1,0:T(2,128)S(1)}, f32[2,12,2,128]{3,2,1,0:T(2,128)S(1)}, u32[]{:S(2)}, u32[]{:S(2)}) collective-permute-start(f32[2,12,2,128]{3,2,1,0:T(2,128)S(1)} %get-tuple-element.77), channel_id=1, source_target_pairs={{1,0},{2,1},{3,2},{5,4},{6,5},{7,6},{9,8},{10,9},{11,10},{13,12},{... | collective-permute-start | bytes 73736 | tf_op jit(solution)/shard_map/ppermute | solution.py:23
  22.7 4.1 %collective-permute-start.2 = (f32[9,16,4,128]{3,2,1,0:T(4,128)S(1)}, f32[9,16,4,128]{3,2,1,0:T(4,128)S(1)}, u32[]{:S(2)}, u32[]{:S(2)}) collective-permute-start(f32[9,16,4,128]{3,2,1,0:T(4,128)S(1)} %get-tuple-element.55), channel_id=1, source_target_pairs={{0,1},{1,2},{2,3},{4,5},{5,6},{6,7},{8,9},{9,10},{10,11},{12,13},{... | collective-permute-start | bytes 884744 | tf_op jit(solution)/shard_map/ppermute | solution.py:20
  26.8 1.9 %collective-permute-start.3 = (f32[9,16,4,128]{3,2,1,0:T(4,128)S(1)}, f32[9,16,4,128]{3,2,1,0:T(4,128)S(1)}, u32[]{:S(2)}, u32[]{:S(2)}) collective-permute-start(f32[9,16,4,128]{3,2,1,0:T(4,128)S(1)} %get-tuple-element.56), channel_id=1, source_target_pairs={{1,0},{2,1},{3,2},{5,4},{6,5},{7,6},{9,8},{10,9},{11,10},{13,12},{... | collective-permute-start | bytes 884744 | tf_op jit(solution)/shard_map/ppermute | solution.py:23
  28.8 1.6 %collective-permute-done.2 = f32[9,16,4,128]{3,2,1,0:T(4,128)S(1)} collective-permute-done((f32[9,16,4,128]{3,2,1,0:T(4,128)S(1)}, f32[9,16,4,128]{3,2,1,0:T(4,128)S(1)}, u32[]{:S(2)}, u32[]{:S(2)}) %collective-permute-start.2) | collective-permute-done | bytes 294944 | tf_op jit(solution)/shard_map/ppermute | solution.py:20
  30.4 4.4 %collective-permute-done.3 = f32[9,16,4,128]{3,2,1,0:T(4,128)S(1)} collective-permute-done((f32[9,16,4,128]{3,2,1,0:T(4,128)S(1)}, f32[9,16,4,128]{3,2,1,0:T(4,128)S(1)}, u32[]{:S(2)}, u32[]{:S(2)}) %collective-permute-start.3) | collective-permute-done | bytes 294944 | tf_op jit(solution)/shard_map/ppermute | solution.py:23
  39.7 4.5 %collective-permute-start.8 = (f32[9,4,8,128]{3,2,1,0:T(8,128)S(1)}, f32[9,4,8,128]{3,2,1,0:T(8,128)S(1)}, u32[]{:S(2)}, u32[]{:S(2)}) collective-permute-start(f32[9,4,8,128]{3,2,1,0:T(8,128)S(1)} %get-tuple-element.65), channel_id=1, source_target_pairs={{0,4},{4,8},{8,12},{12,16},{16,20},{20,24},{24,28},{1,5},{5,9},{9,... | collective-permute-start | bytes 442376 | tf_op jit(solution)/shard_map/ppermute | solution.py:20
  44.2 1.3 %collective-permute-start.9 = (f32[9,4,8,128]{3,2,1,0:T(8,128)S(1)}, f32[9,4,8,128]{3,2,1,0:T(8,128)S(1)}, u32[]{:S(2)}, u32[]{:S(2)}) collective-permute-start(f32[9,4,8,128]{3,2,1,0:T(8,128)S(1)} %get-tuple-element.66), channel_id=1, source_target_pairs={{4,0},{8,4},{12,8},{16,12},{20,16},{24,20},{28,24},{5,1},{9,5},{13... | collective-permute-start | bytes 442376 | tf_op jit(solution)/shard_map/ppermute | solution.py:23
  46.3 4.7 %collective-permute-done.9 = f32[9,4,8,128]{3,2,1,0:T(8,128)S(1)} collective-permute-done((f32[9,4,8,128]{3,2,1,0:T(8,128)S(1)}, f32[9,4,8,128]{3,2,1,0:T(8,128)S(1)}, u32[]{:S(2)}, u32[]{:S(2)}) %collective-permute-start.9) | collective-permute-done | bytes 147488 | tf_op jit(solution)/shard_map/ppermute | solution.py:23
  51.1 2.9 %collective-permute-start.10 = (f32[9,16,4,128]{3,2,1,0:T(4,128)S(1)}, f32[9,16,4,128]{3,2,1,0:T(4,128)S(1)}, u32[]{:S(2)}, u32[]{:S(2)}) collective-permute-start(f32[9,16,4,128]{3,2,1,0:T(4,128)S(1)} %get-tuple-element.53), channel_id=1, source_target_pairs={{0,1},{1,2},{2,3},{4,5},{5,6},{6,7},{8,9},{9,10},{10,11},{12,13},{... | collective-permute-start | bytes 884744 | tf_op jit(solution)/shard_map/ppermute | solution.py:20
  54.0 1.9 %collective-permute-start.11 = (f32[9,16,4,128]{3,2,1,0:T(4,128)S(1)}, f32[9,16,4,128]{3,2,1,0:T(4,128)S(1)}, u32[]{:S(2)}, u32[]{:S(2)}) collective-permute-start(f32[9,16,4,128]{3,2,1,0:T(4,128)S(1)} %get-tuple-element.54), channel_id=1, source_target_pairs={{1,0},{2,1},{3,2},{5,4},{6,5},{7,6},{9,8},{10,9},{11,10},{13,12},{... | collective-permute-start | bytes 884744 | tf_op jit(solution)/shard_map/ppermute | solution.py:23
  55.9 1.7 %collective-permute-done.10 = f32[9,16,4,128]{3,2,1,0:T(4,128)S(1)} collective-permute-done((f32[9,16,4,128]{3,2,1,0:T(4,128)S(1)}, f32[9,16,4,128]{3,2,1,0:T(4,128)S(1)}, u32[]{:S(2)}, u32[]{:S(2)}) %collective-permute-start.10) | collective-permute-done | bytes 294944 | tf_op jit(solution)/shard_map/ppermute | solution.py:20
  57.6 4.4 %collective-permute-done.11 = f32[9,16,4,128]{3,2,1,0:T(4,128)S(1)} collective-permute-done((f32[9,16,4,128]{3,2,1,0:T(4,128)S(1)}, f32[9,16,4,128]{3,2,1,0:T(4,128)S(1)}, u32[]{:S(2)}, u32[]{:S(2)}) %collective-permute-start.11) | collective-permute-done | bytes 294944 | tf_op jit(solution)/shard_map/ppermute | solution.py:23
  66.4 4.5 %collective-permute-start.12 = (f32[9,4,8,128]{3,2,1,0:T(8,128)S(1)}, f32[9,4,8,128]{3,2,1,0:T(8,128)S(1)}, u32[]{:S(2)}, u32[]{:S(2)}) collective-permute-start(f32[9,4,8,128]{3,2,1,0:T(8,128)S(1)} %get-tuple-element.60), channel_id=1, source_target_pairs={{0,4},{4,8},{8,12},{12,16},{16,20},{20,24},{24,28},{1,5},{5,9},{9,... | collective-permute-start | bytes 442376 | tf_op jit(solution)/shard_map/ppermute | solution.py:20
  71.0 1.3 %collective-permute-start.13 = (f32[9,4,8,128]{3,2,1,0:T(8,128)S(1)}, f32[9,4,8,128]{3,2,1,0:T(8,128)S(1)}, u32[]{:S(2)}, u32[]{:S(2)}) collective-permute-start(f32[9,4,8,128]{3,2,1,0:T(8,128)S(1)} %get-tuple-element.61), channel_id=1, source_target_pairs={{4,0},{8,4},{12,8},{16,12},{20,16},{24,20},{28,24},{5,1},{9,5},{13... | collective-permute-start | bytes 442376 | tf_op jit(solution)/shard_map/ppermute | solution.py:23
  73.5 3.4 %collective-permute-done.13 = f32[9,4,8,128]{3,2,1,0:T(8,128)S(1)} collective-permute-done((f32[9,4,8,128]{3,2,1,0:T(8,128)S(1)}, f32[9,4,8,128]{3,2,1,0:T(8,128)S(1)}, u32[]{:S(2)}, u32[]{:S(2)}) %collective-permute-start.13) | collective-permute-done | bytes 147488 | tf_op jit(solution)/shard_map/ppermute | solution.py:23
  77.0 1.9 %collective-permute-start.15 = (f32[9,16,4,128]{3,1,2,0:T(8,128)S(1)}, f32[9,16,4,128]{3,1,2,0:T(8,128)S(1)}, u32[]{:S(2)}, u32[]{:S(2)}) collective-permute-start(f32[9,16,4,128]{3,1,2,0:T(8,128)S(1)} %copy.31), channel_id=1, source_target_pairs={{1,0},{2,1},{3,2},{5,4},{6,5},{7,6},{9,8},{10,9},{11,10},{13,12},{... | collective-permute-start | bytes 884744 | tf_op jit(solution)/shard_map/ppermute | solution.py:23
  79.0 3.8 %collective-permute-start.14 = (f32[9,16,4,128]{3,1,2,0:T(8,128)S(1)}, f32[9,16,4,128]{3,1,2,0:T(8,128)S(1)}, u32[]{:S(2)}, u32[]{:S(2)}) collective-permute-start(f32[9,16,4,128]{3,1,2,0:T(8,128)S(1)} %copy.30), channel_id=1, source_target_pairs={{0,1},{1,2},{2,3},{4,5},{5,6},{6,7},{8,9},{9,10},{10,11},{12,13},{... | collective-permute-start | bytes 884744 | tf_op jit(solution)/shard_map/ppermute | solution.py:20
  82.8 2.3 %collective-permute-done.15 = f32[9,16,4,128]{3,1,2,0:T(8,128)S(1)} collective-permute-done((f32[9,16,4,128]{3,1,2,0:T(8,128)S(1)}, f32[9,16,4,128]{3,1,2,0:T(8,128)S(1)}, u32[]{:S(2)}, u32[]{:S(2)}) %collective-permute-start.15) | collective-permute-done | bytes 294944 | tf_op jit(solution)/shard_map/ppermute | solution.py:23
  (106 shorter events, 21.8 us)
Async XLA Ops:
  0.6 9.9 %copy-start.3 = (f32[6]{0:T(128)S(1)}, f32[6]{0:T(128)}, u32[]{:S(2)}) copy-start(f32[6]{0:T(128)} %constant.16.clone) | copy-start | bytes 76
  0.6 9.9 %copy-start.2 = (f32[8,8,128]{2,1,0:T(8,128)S(1)}, f32[8,8,128]{2,1,0:T(8,128)}, u32[]{:S(2)}) copy-start(f32[8,8,128]{2,1,0:T(8,128)} %param.13) | copy-start | bytes 98308
  0.7 10.0 %copy-start.1 = (f32[3,8,8,128]{3,2,1,0:T(8,128)S(1)}, f32[3,8,8,128]{3,2,1,0:T(8,128)}, u32[]{:S(2)}) copy-start(f32[3,8,8,128]{3,2,1,0:T(8,128)} %param.11) | copy-start | bytes 294916
  3.5 12.4 %copy-start.4 = (f32[8,8]{1,0:T(8,128)S(1)}, f32[8,8]{1,0:T(8,128)}, u32[]{:S(2)}) copy-start(f32[8,8]{1,0:T(8,128)} %param.17) | copy-start | bytes 772
  3.7 12.3 %collective-permute-start.4 = (f32[2,2,8,128]{3,2,1,0:T(8,128)S(1)}, f32[2,2,8,128]{3,2,1,0:T(8,128)S(1)}, u32[]{:S(2)}, u32[]{:S(2)}) collective-permute-start(f32[2,2,8,128]{3,2,1,0:T(8,128)S(1)} %get-tuple-element.78), channel_id=1, source_target_pairs={{0,4},{4,8},{8,12},{12,16},{16,20},{20,24},{24,28},{1,5},{5,9},{9,... | collective-permute-start | bytes 49160 | tf_op jit(solution)/shard_map/ppermute | solution.py:20
  7.7 8.3 %collective-permute-start.5 = (f32[2,2,8,128]{3,2,1,0:T(8,128)S(1)}, f32[2,2,8,128]{3,2,1,0:T(8,128)S(1)}, u32[]{:S(2)}, u32[]{:S(2)}) collective-permute-start(f32[2,2,8,128]{3,2,1,0:T(8,128)S(1)} %get-tuple-element.79), channel_id=1, source_target_pairs={{4,0},{8,4},{12,8},{16,12},{20,16},{24,20},{28,24},{5,1},{9,5},{13... | collective-permute-start | bytes 49160 | tf_op jit(solution)/shard_map/ppermute | solution.py:23
  10.6 11.8 %collective-permute-start = (f32[9,4,8,128]{3,2,1,0:T(8,128)S(1)}, f32[9,4,8,128]{3,2,1,0:T(8,128)S(1)}, u32[]{:S(2)}, u32[]{:S(2)}) collective-permute-start(f32[9,4,8,128]{3,2,1,0:T(8,128)S(1)} %get-tuple-element.70), channel_id=1, source_target_pairs={{0,4},{4,8},{8,12},{12,16},{16,20},{20,24},{24,28},{1,5},{5,9},{9,... | collective-permute-start | bytes 442376 | tf_op jit(solution)/shard_map/ppermute | solution.py:20
  14.6 7.8 %collective-permute-start.1 = (f32[9,4,8,128]{3,2,1,0:T(8,128)S(1)}, f32[9,4,8,128]{3,2,1,0:T(8,128)S(1)}, u32[]{:S(2)}, u32[]{:S(2)}) collective-permute-start(f32[9,4,8,128]{3,2,1,0:T(8,128)S(1)} %get-tuple-element.71), channel_id=1, source_target_pairs={{4,0},{8,4},{12,8},{16,12},{20,16},{24,20},{28,24},{5,1},{9,5},{13... | collective-permute-start | bytes 442376 | tf_op jit(solution)/shard_map/ppermute | solution.py:23
  16.0 12.7 %collective-permute-start.6 = (f32[2,12,2,128]{3,2,1,0:T(2,128)S(1)}, f32[2,12,2,128]{3,2,1,0:T(2,128)S(1)}, u32[]{:S(2)}, u32[]{:S(2)}) collective-permute-start(f32[2,12,2,128]{3,2,1,0:T(2,128)S(1)} %get-tuple-element.76), channel_id=1, source_target_pairs={{0,1},{1,2},{2,3},{4,5},{5,6},{6,7},{8,9},{9,10},{10,11},{12,13},{... | collective-permute-start | bytes 73736 | tf_op jit(solution)/shard_map/ppermute | solution.py:20
  20.5 8.2 %collective-permute-start.7 = (f32[2,12,2,128]{3,2,1,0:T(2,128)S(1)}, f32[2,12,2,128]{3,2,1,0:T(2,128)S(1)}, u32[]{:S(2)}, u32[]{:S(2)}) collective-permute-start(f32[2,12,2,128]{3,2,1,0:T(2,128)S(1)} %get-tuple-element.77), channel_id=1, source_target_pairs={{1,0},{2,1},{3,2},{5,4},{6,5},{7,6},{9,8},{10,9},{11,10},{13,12},{... | collective-permute-start | bytes 73736 | tf_op jit(solution)/shard_map/ppermute | solution.py:23
  22.7 7.8 %collective-permute-start.2 = (f32[9,16,4,128]{3,2,1,0:T(4,128)S(1)}, f32[9,16,4,128]{3,2,1,0:T(4,128)S(1)}, u32[]{:S(2)}, u32[]{:S(2)}) collective-permute-start(f32[9,16,4,128]{3,2,1,0:T(4,128)S(1)} %get-tuple-element.55), channel_id=1, source_target_pairs={{0,1},{1,2},{2,3},{4,5},{5,6},{6,7},{8,9},{9,10},{10,11},{12,13},{... | collective-permute-start | bytes 884744 | tf_op jit(solution)/shard_map/ppermute | solution.py:20
  26.8 8.0 %collective-permute-start.3 = (f32[9,16,4,128]{3,2,1,0:T(4,128)S(1)}, f32[9,16,4,128]{3,2,1,0:T(4,128)S(1)}, u32[]{:S(2)}, u32[]{:S(2)}) collective-permute-start(f32[9,16,4,128]{3,2,1,0:T(4,128)S(1)} %get-tuple-element.56), channel_id=1, source_target_pairs={{1,0},{2,1},{3,2},{5,4},{6,5},{7,6},{9,8},{10,9},{11,10},{13,12},{... | collective-permute-start | bytes 884744 | tf_op jit(solution)/shard_map/ppermute | solution.py:23
  37.1 1.4 %copy-start = (f32[8,6,8,8,128]{4,3,2,1,0:T(8,128)S(1)}, f32[8,6,8,8,128]{4,3,2,1,0:T(8,128)}, u32[]{:S(2)}) copy-start(f32[8,6,8,8,128]{4,3,2,1,0:T(8,128)} %param.12) | copy-start | bytes 4718596
  39.7 6.6 %collective-permute-start.8 = (f32[9,4,8,128]{3,2,1,0:T(8,128)S(1)}, f32[9,4,8,128]{3,2,1,0:T(8,128)S(1)}, u32[]{:S(2)}, u32[]{:S(2)}) collective-permute-start(f32[9,4,8,128]{3,2,1,0:T(8,128)S(1)} %get-tuple-element.65), channel_id=1, source_target_pairs={{0,4},{4,8},{8,12},{12,16},{16,20},{20,24},{24,28},{1,5},{5,9},{9,... | collective-permute-start | bytes 442376 | tf_op jit(solution)/shard_map/ppermute | solution.py:20
  44.2 6.7 %collective-permute-start.9 = (f32[9,4,8,128]{3,2,1,0:T(8,128)S(1)}, f32[9,4,8,128]{3,2,1,0:T(8,128)S(1)}, u32[]{:S(2)}, u32[]{:S(2)}) collective-permute-start(f32[9,4,8,128]{3,2,1,0:T(8,128)S(1)} %get-tuple-element.66), channel_id=1, source_target_pairs={{4,0},{8,4},{12,8},{16,12},{20,16},{24,20},{28,24},{5,1},{9,5},{13... | collective-permute-start | bytes 442376 | tf_op jit(solution)/shard_map/ppermute | solution.py:23
  51.1 6.6 %collective-permute-start.10 = (f32[9,16,4,128]{3,2,1,0:T(4,128)S(1)}, f32[9,16,4,128]{3,2,1,0:T(4,128)S(1)}, u32[]{:S(2)}, u32[]{:S(2)}) collective-permute-start(f32[9,16,4,128]{3,2,1,0:T(4,128)S(1)} %get-tuple-element.53), channel_id=1, source_target_pairs={{0,1},{1,2},{2,3},{4,5},{5,6},{6,7},{8,9},{9,10},{10,11},{12,13},{... | collective-permute-start | bytes 884744 | tf_op jit(solution)/shard_map/ppermute | solution.py:20
  54.0 8.0 %collective-permute-start.11 = (f32[9,16,4,128]{3,2,1,0:T(4,128)S(1)}, f32[9,16,4,128]{3,2,1,0:T(4,128)S(1)}, u32[]{:S(2)}, u32[]{:S(2)}) collective-permute-start(f32[9,16,4,128]{3,2,1,0:T(4,128)S(1)} %get-tuple-element.54), channel_id=1, source_target_pairs={{1,0},{2,1},{3,2},{5,4},{6,5},{7,6},{9,8},{10,9},{11,10},{13,12},{... | collective-permute-start | bytes 884744 | tf_op jit(solution)/shard_map/ppermute | solution.py:23
  66.4 7.0 %collective-permute-start.12 = (f32[9,4,8,128]{3,2,1,0:T(8,128)S(1)}, f32[9,4,8,128]{3,2,1,0:T(8,128)S(1)}, u32[]{:S(2)}, u32[]{:S(2)}) collective-permute-start(f32[9,4,8,128]{3,2,1,0:T(8,128)S(1)} %get-tuple-element.60), channel_id=1, source_target_pairs={{0,4},{4,8},{8,12},{12,16},{16,20},{20,24},{24,28},{1,5},{5,9},{9,... | collective-permute-start | bytes 442376 | tf_op jit(solution)/shard_map/ppermute | solution.py:20
  71.0 5.9 %collective-permute-start.13 = (f32[9,4,8,128]{3,2,1,0:T(8,128)S(1)}, f32[9,4,8,128]{3,2,1,0:T(8,128)S(1)}, u32[]{:S(2)}, u32[]{:S(2)}) collective-permute-start(f32[9,4,8,128]{3,2,1,0:T(8,128)S(1)} %get-tuple-element.61), channel_id=1, source_target_pairs={{4,0},{8,4},{12,8},{16,12},{20,16},{24,20},{28,24},{5,1},{9,5},{13... | collective-permute-start | bytes 442376 | tf_op jit(solution)/shard_map/ppermute | solution.py:23
  77.0 8.0 %collective-permute-start.15 = (f32[9,16,4,128]{3,1,2,0:T(8,128)S(1)}, f32[9,16,4,128]{3,1,2,0:T(8,128)S(1)}, u32[]{:S(2)}, u32[]{:S(2)}) collective-permute-start(f32[9,16,4,128]{3,1,2,0:T(8,128)S(1)} %copy.31), channel_id=1, source_target_pairs={{1,0},{2,1},{3,2},{5,4},{6,5},{7,6},{9,8},{10,9},{11,10},{13,12},{... | collective-permute-start | bytes 884744 | tf_op jit(solution)/shard_map/ppermute | solution.py:23
  79.0 7.3 %collective-permute-start.14 = (f32[9,16,4,128]{3,1,2,0:T(8,128)S(1)}, f32[9,16,4,128]{3,1,2,0:T(8,128)S(1)}, u32[]{:S(2)}, u32[]{:S(2)}) collective-permute-start(f32[9,16,4,128]{3,1,2,0:T(8,128)S(1)} %copy.30), channel_id=1, source_target_pairs={{0,1},{1,2},{2,3},{4,5},{5,6},{6,7},{8,9},{9,10},{10,11},{12,13},{... | collective-permute-start | bytes 884744 | tf_op jit(solution)/shard_map/ppermute | solution.py:20
where the time goes:
time: 93.1 us; the launch traced here: 92.4 us
  starting transfers between devices  45.3 us (49%)
  waiting for transfers between devices  25.5 us (27%)
  other arithmetic  16 us (17%)
  local copies, waits for them, and re-layouts  4.24 us (5%)
  between operations  1.4 us (2%)
    ppermute x8, starting transfers between devices, with_halo(): lax.ppermute(lax.slice_in_dim(block, block.shape[dim] - width, None, axis...  32.4 us
    ppermute x8, waiting for transfers between devices, with_halo(): lax.ppermute(lax.slice_in_dim(block, 0, width, axis=dim), axis, backward)  19.1 us
    ppermute x8, starting transfers between devices, with_halo(): lax.ppermute(lax.slice_in_dim(block, 0, width, axis=dim), axis, backward)  12.9 us
    ppermute x8, waiting for transfers between devices, with_halo(): lax.ppermute(lax.slice_in_dim(block, block.shape[dim] - width, None, axis...  6.41 us
    another operation x9, other arithmetic, advance(): jnp.stack([forward(stress_pad[0], 0) + backward(stress_pad[3], 1) + backw...  3.23 us
    concatenate x7, other arithmetic, with_halo(): block = jnp.concatenate([low, block, high], axis=dim)  2.8 us
    reduce_sum x4, other arithmetic, total_stress(): return jnp.sum(surfaces, axis=0) + diagonal_mask * mean_stress[None]  2.5 us
  transfers between devices with their start and end apart: 16, of which 10 were waited for; matrix products, arithmetic and copies ran while one was open for 2% of the time, Pallas kernels for 0%

commit v1 on v0

v1 whole, which is shorter than its diff:
```python
import functools

import jax
import jax.numpy as jnp
from jax import lax
from jax.experimental import pallas as pl
from jax.experimental.pallas import tpu as pltpu
from jax.sharding import PartitionSpec as P

ITERS = 3
SURF = 8
ZONES = 8
C1 = 9.0 / 8.0
C2 = -1.0 / 24.0
DT = 0.1
SPONGE = 0.1

B = 8
WX = 12
WY = 16
XX, YY, ZZ, XY, XZ, YZ = range(6)

NORMAL = ((XX, XY, XZ), (YY, XY, YZ))
ALONG = ((XY, YY, YZ), (XY, XX, XZ))
VELOCITY = ((0, 1, 2), (1, 0, 2))

FACES = ((0, -1), (0, 1), (1, -1), (1, 1))
CORNERS = ((-1, -1), (-1, 1), (1, -1), (1, 1))


def kernel(
    nx, ny,
    velocity, surfaces, mean_in, zone, sponge, moduli, yields,
    velocity_out, stress_out,
    surf, mean, S, V, A, D, bulk, shear, limit, strips,
    face_out, face_in, corner_out, corner_in,
    load_sem, face_send, face_recv, corner_send, corner_recv,
):
    px, py = lax.axis_index("gx"), lax.axis_index("gy")
    f32 = jnp.float32

    load_surf = pltpu.make_async_copy(surfaces, surf, load_sem.at[0])
    load_surf.start()

    def has(axis, side):
        at, count = ((px, nx), (py, ny))[axis]
        return at > 0 if side < 0 else at < count - 1

    def has_corner(dx, dy):
        return jnp.logical_and(has(0, dx), has(1, dy))

    def device(dx, dy):
        return (px + dx, py + dy)

    barrier = pltpu.get_barrier_semaphore()
    neighbours = [((dx, 0), has(0, dx)) for dx in (-1, 1)]
    neighbours += [((0, dy), has(1, dy)) for dy in (-1, 1)]
    neighbours += [(d, has_corner(*d)) for d in CORNERS]
    for (dx, dy), there in neighbours:
        @pl.when(there)
        def _():
            pl.semaphore_signal(
                barrier, inc=1, device_id=device(dx, dy),
                device_id_type=pl.DeviceIdType.MESH,
            )

    zero = jnp.zeros((B, 128), f32)

    for axis, side in FACES:
        @pl.when(jnp.logical_not(has(axis, side)))
        def _():
            for t in range(ITERS):
                for tile in range(11):
                    face_in[t, axis, (side + 1) // 2, tile] = zero
    for index, (dx, dy) in enumerate(CORNERS):
        @pl.when(jnp.logical_not(has_corner(dx, dy)))
        def _():
            for t in range(ITERS):
                for part in range(3):
                    corner_in[t, index, part * 8:part * 8 + 8, :] = zero

    @pl.loop(0, 6 * WX)
    def _(i):
        S[i, 0:8, :] = zero
        S[i, 8:16, :] = zero

    @pl.loop(0, 24)
    def _(i):
        strips[i, 0:8, :] = zero
        strips[i, 8:16, :] = zero

    def pick(table, column, b0, b1, b2):
        v = [table[z, column] for z in range(ZONES)]
        a = [jnp.where(b0, v[2 * n + 1], v[2 * n]) for n in range(4)]
        c = [jnp.where(b1, a[2 * n + 1], a[2 * n]) for n in range(2)]
        return jnp.where(b2, c[1], c[0])

    @pl.loop(0, B)
    def _(i):
        z = zone[i]
        b0, b1, b2 = (z & 1) > 0, (z & 2) > 0, (z & 4) > 0
        damping = 1.0 - SPONGE * sponge[i].astype(f32)
        bulk[i] = DT * pick(moduli, 0, b0, b1, b2)
        shear[i] = (2.0 * DT / SURF) * pick(moduli, 1, b0, b1, b2)
        A[i] = DT * pick(moduli, 2, b0, b1, b2) * damping
        D[i] = damping
        for k in range(SURF):
            limit[k, i] = pick(yields, k, b0, b1, b2)
        mean[i] = mean_in[i]
        for c in range(3):
            V[c * WX + 2 + i, 4:12, :] = velocity[c, i]

    lane = lax.broadcasted_iota(jnp.int32, (B, 128), 1)

    def mask(keep, value):
        return jnp.where(keep, f32(value), f32(0))

    f_up1 = mask(lane < 127, C1)
    f_up2 = mask(lane < 126, C2)
    f_dn1 = mask(lane >= 1, C2)
    b_dn1 = mask(lane >= 1, C1)
    b_up1 = mask(lane < 127, C2)
    b_dn2 = mask(lane >= 2, C2)

    def forward_z(f):
        return (
            f_up1 * pltpu.roll(f, 127, 1) - C1 * f
            + f_up2 * pltpu.roll(f, 126, 1) - f_dn1 * pltpu.roll(f, 1, 1)
        )

    def backward_z(f):
        return (
            C1 * f - b_dn1 * pltpu.roll(f, 1, 1)
            + b_up1 * pltpu.roll(f, 127, 1) - b_dn2 * pltpu.roll(f, 2, 1)
        )

    def forward_of(at):
        return C1 * (at(1) - at(0)) + C2 * (at(2) - at(-1))

    def backward_of(at):
        return C1 * (at(0) - at(-1)) + C2 * (at(1) - at(-2))

    def along_x(ref, c, i):
        return lambda o: ref[c * WX + 2 + i + o, 4:12, :]

    def along_rows(ref, n):
        return lambda o: ref[n, 4 + o:12 + o, :]

    def along_y(ref, c, i):
        return along_rows(ref, c * WX + 2 + i)

    S_rows = S.reshape(6 * WX * WY, 128)
    V_rows = V.reshape(3 * WX * WY, 128)
    A_rows = A.reshape(B * B, 128)

    def rows_of(c, k):
        return (pl.ds((c * WX + 2) * WY + 4 + k, B, stride=WY), slice(None))

    def get_s(axis, c, k):
        return S[c * WX + 2 + k, 4:12, :] if axis == 0 else S_rows[rows_of(c, k)]

    def get_v(axis, c, k):
        return V[c * WX + 2 + k, 4:12, :] if axis == 0 else V_rows[rows_of(c, k)]

    def set_v(axis, c, k, value):
        if axis == 0:
            V[c * WX + 2 + k, 4:12, :] = value
        else:
            V_rows[rows_of(c, k)] = value

    def get_a(axis, k):
        return A[k] if axis == 0 else A_rows[pl.ds(k, B, stride=B), :]

    def face_copy(t, axis, side, toward):
        own, other = (side + 1) // 2, (1 - side) // 2
        tiles = pl.ds(0, 11 if t == 0 else 9)
        shift = (toward, 0) if axis == 0 else (0, toward)
        return pltpu.make_async_remote_copy(
            src_ref=face_out.at[t, axis, own, tiles],
            dst_ref=face_in.at[t, axis, other, tiles],
            send_sem=face_send.at[t, axis, own],
            recv_sem=face_recv.at[t, axis, other],
            device_id=device(*shift),
            device_id_type=pl.DeviceIdType.MESH,
        )

    def corner_copy(t, index, toward):
        dx, dy = CORNERS[toward]
        return pltpu.make_async_remote_copy(
            src_ref=corner_out.at[t, index],
            dst_ref=corner_in.at[t, 3 - index],
            send_sem=corner_send.at[t, index],
            recv_sem=corner_recv.at[t, 3 - index],
            device_id=device(dx, dy),
            device_id_type=pl.DeviceIdType.MESH,
        )

    def send_corners(t):
        for index, (dx, dy) in enumerate(CORNERS):
            kx, ky = (6 if dx > 0 else 0), (6 if dy > 0 else 0)
            for n in range(3):
                for k in range(2):
                    row = (n * 2 + k) * 2
                    corner_out[t, index, row:row + 2, :] = S[
                        ALONG[0][n] * WX + 2 + kx + k, 4 + ky:6 + ky, :
                    ]
                    for m in range(2):
                        corner_out[t, index, 12 + row + m:13 + row + m, :] = S[
                            ALONG[1][n] * WX + 2 + kx + m, 4 + ky + k:5 + ky + k, :
                        ]

            @pl.when(has_corner(dx, dy))
            def _():
                corner_copy(t, index, index).start()

    def send_faces(t):
        for axis, side in FACES:
            n, tg, z = NORMAL[axis]
            vn, vt, vz = VELOCITY[axis]
            s = functools.partial(get_s, axis)
            v = functools.partial(get_v, axis)
            if side > 0:
                tiles = [s(n, 7), s(tg, 6), s(tg, 7), s(z, 6), s(z, 7),
                         v(vn, 6), v(vn, 7), v(vt, 7), v(vz, 7)]
                a_from = 6
            else:
                tiles = [s(n, 0), s(n, 1), s(tg, 0), s(z, 0),
                         v(vn, 0), v(vt, 0), v(vt, 1), v(vz, 0), v(vz, 1)]
                a_from = 0
            if t == 0:
                tiles += [get_a(axis, a_from), get_a(axis, a_from + 1)]
            for index, tile in enumerate(tiles):
                face_out[t, axis, (side + 1) // 2, index] = tile

            @pl.when(has(axis, side))
            def _():
                face_copy(t, axis, side, side).start()

    def partial_velocity():
        @pl.loop(0, B)
        def _(i):
            sx = functools.partial(along_x, S)
            sy = functools.partial(along_y, S)
            here = lambda c: S[c * WX + 2 + i, 4:12, :]
            accel = (
                forward_of(sx(XX, i)) + backward_of(sy(XY, i)) + backward_z(here(XZ)),
                backward_of(sx(XY, i)) + forward_of(sy(YY, i)) + backward_z(here(YZ)),
                backward_of(sx(XZ, i)) + backward_of(sy(YZ, i)) + forward_z(here(ZZ)),
            )
            for c in range(3):
                V[c * WX + 2 + i, 4:12, :] = (
                    D[i] * V[c * WX + 2 + i, 4:12, :] + A[i] * accel[c]
                )

    def receive(t):
        for axis, side in FACES:
            @pl.when(has(axis, side))
            def _():
                face_copy(t, axis, -side, side).wait_recv()
        for index, (dx, dy) in enumerate(CORNERS):
            @pl.when(has_corner(dx, dy))
            def _():
                corner_copy(t, 3 - index, index).wait_recv()

    def finish_velocity(t):
        for index, (dx, dy) in enumerate(CORNERS):
            for axis, side, other in ((0, dx, dy), (1, dy, dx)):
                at = 2 if other < 0 else 12
                for n in range(6):
                    row = axis * 12 + n * 2
                    strips[(axis * 2 + (side + 1) // 2) * 6 + n, at:at + 2, :] = (
                        corner_in[t, index, row:row + 2, :]
                    )
        for axis in range(2):
            n, tg, z = NORMAL[axis]
            vn, vt, vz = VELOCITY[axis]
            s = functools.partial(get_s, axis)
            a = functools.partial(get_a, axis)

            def add(c, k, value):
                set_v(axis, c, k, get_v(axis, c, k) + a(k) * value)

            def strip(side, m, k):
                return along_rows(strips, (axis * 2 + side) * 6 + m * 2 + k)

            lo = lambda m: face_in[t, axis, 0, m]
            hi = lambda m: face_in[t, axis, 1, m]
            a_lo = lambda k: face_in[0, axis, 0, 9 + k]
            a_hi = lambda k: face_in[0, axis, 1, 9 + k]

            set_v(axis, vn, -2, lo(5) + a_lo(0) * (
                C2 * s(n, 0) + backward_of(strip(0, 0, 0))))
            set_v(axis, vn, -1, lo(6) + a_lo(1) * (
                C1 * s(n, 0) + C2 * s(n, 1) + backward_of(strip(0, 0, 1))))
            set_v(axis, vt, -1, lo(7) + a_lo(1) * (
                C2 * s(tg, 0) + forward_of(strip(0, 1, 1))))
            set_v(axis, vz, -1, lo(8) + a_lo(1) * (
                C2 * s(z, 0) + backward_of(strip(0, 2, 1))))
            set_v(axis, vn, 8, hi(4) + a_hi(0) * (
                -C2 * s(n, 7) + backward_of(strip(1, 0, 0))))
            set_v(axis, vt, 8, hi(5) + a_hi(0) * (
                -C1 * s(tg, 7) - C2 * s(tg, 6) + forward_of(strip(1, 1, 0))))
            set_v(axis, vt, 9, hi(6) + a_hi(1) * (
                -C2 * s(tg, 7) + forward_of(strip(1, 1, 1))))
            set_v(axis, vz, 8, hi(7) + a_hi(0) * (
                -C1 * s(z, 7) - C2 * s(z, 6) + backward_of(strip(1, 2, 0))))
            set_v(axis, vz, 9, hi(8) + a_hi(1) * (
                -C2 * s(z, 7) + backward_of(strip(1, 2, 1))))

            add(vn, 0, -C2 * lo(0))
            add(vn, 6, C2 * hi(0))
            add(vn, 7, C1 * hi(0) + C2 * hi(1))
            for c, m, h in ((vt, 1, 2), (vz, 3, 3)):
                add(c, 0, -C1 * lo(m + 1) - C2 * lo(m))
                add(c, 1, -C2 * lo(m + 1))
                add(c, 7, C2 * hi(h))

    def plastic():
        @pl.loop(0, B)
        def _(i):
            vx = functools.partial(along_x, V)
            vy = functools.partial(along_y, V)
            here = lambda c: V[c * WX + 2 + i, 4:12, :]
            xx = backward_of(vx(0, i))
            yy = backward_of(vy(1, i))
            zz = backward_z(here(2))
            trace = xx + yy + zz
            third = trace * (1.0 / 3.0)
            g = shear[i]
            h = 0.5 * g
            move = (
                g * (xx - third), g * (yy - third), g * (zz - third),
                h * (forward_of(vy(0, i)) + forward_of(vx(1, i))),
                h * (forward_z(here(0)) + forward_of(vx(2, i))),
                h * (forward_z(here(1)) + forward_of(vy(2, i))),
            )
            pressure = mean[i] + bulk[i] * trace
            mean[i] = pressure
            total = [None] * 6
            for k in range(SURF):
                trial = [surf[k, c, i] + move[c] for c in range(6)]
                sq = [f * f for f in trial]
                size2 = 0.5 * (sq[0] + sq[1] + sq[2]) + (sq[3] + sq[4] + sq[5])
                lim = limit[k, i]
                factor = lim * lax.rsqrt(jnp.maximum(size2, lim * lim))
                for c in range(6):
                    new = trial[c] * factor
                    surf[k, c, i] = new
                    total[c] = new if k == 0 else total[c] + new
            for c in range(6):
                S[c * WX + 2 + i, 4:12, :] = total[c] + pressure if c < 3 else total[c]

    load_surf.wait()

    @pl.loop(0, B)
    def _(i):
        for c in range(6):
            total = surf[0, c, i]
            for k in range(1, SURF):
                total = total + surf[k, c, i]
            S[c * WX + 2 + i, 4:12, :] = total + mean[i] if c < 3 else total

    count = sum(there.astype(jnp.int32) for _, there in neighbours)
    pl.semaphore_wait(barrier, count)

    for t in range(ITERS):
        send_corners(t)
        partial_velocity()
        send_faces(t)
        receive(t)
        finish_velocity(t)
        plastic()

    for c in range(3):
        for i in range(B):
            velocity_out[c, i] = V[c * WX + 2 + i, 4:12, :]
    for c in range(6):
        for i in range(B):
            stress_out[c, i] = S[c * WX + 2 + i, 4:12, :]

    for t in range(ITERS):
        for axis, side in FACES:
            @pl.when(has(axis, side))
            def _():
                face_copy(t, axis, side, side).wait_send()
        for index, (dx, dy) in enumerate(CORNERS):
            @pl.when(has_corner(dx, dy))
            def _():
                corner_copy(t, index, index).wait_send()


def body(nx, ny, velocity, surfaces, mean_stress, zone, sponge, moduli, yields):
    vmem = pl.BlockSpec(memory_space=pltpu.VMEM)
    smem = pl.BlockSpec(memory_space=pltpu.SMEM)
    f32 = jnp.float32
    tiles = lambda *lead: pltpu.VMEM(lead + (B, 128), f32)
    return pl.pallas_call(
        functools.partial(kernel, nx, ny),
        out_shape=(
            jax.ShapeDtypeStruct((3, B, B, 128), f32),
            jax.ShapeDtypeStruct((6, B, B, 128), f32),
        ),
        in_specs=[vmem, pl.BlockSpec(memory_space=pl.ANY), vmem, vmem, vmem, smem, smem],
        out_specs=(vmem, vmem),
        scratch_shapes=[
            tiles(SURF, 6, B),
            tiles(B),
            pltpu.VMEM((6 * WX, WY, 128), f32),
            pltpu.VMEM((3 * WX, WY, 128), f32),
            tiles(B), tiles(B), tiles(B), tiles(B),
            tiles(SURF, B),
            pltpu.VMEM((24, WY, 128), f32),
            tiles(ITERS, 2, 2, 11),
            tiles(ITERS, 2, 2, 11),
            pltpu.VMEM((ITERS, 4, 24, 128), f32),
            pltpu.VMEM((ITERS, 4, 24, 128), f32),
            pltpu.SemaphoreType.DMA((1,)),
            pltpu.SemaphoreType.DMA((ITERS, 2, 2)),
            pltpu.SemaphoreType.DMA((ITERS, 2, 2)),
            pltpu.SemaphoreType.DMA((ITERS, 4)),
            pltpu.SemaphoreType.DMA((ITERS, 4)),
        ],
        compiler_params=pltpu.CompilerParams(
            collective_id=0, has_side_effects=True, vmem_limit_bytes=32 << 20
        ),
    )(velocity, surfaces, mean_stress, zone, sponge, moduli, yields)


def solution(mesh):
    return jax.shard_map(
        functools.partial(body, mesh.shape["gx"], mesh.shape["gy"]),
        mesh=mesh,
        in_specs=(
            P(None, "gx", "gy", None),
            P(None, None, "gx", "gy", None),
            P("gx", "gy", None),
            P("gx", "gy", None),
            P("gx", "gy", None),
            P(),
            P(),
        ),
        out_specs=(P(None, "gx", "gy", None), P(None, "gx", "gy", None)),
        check_vma=False,
    )
```

time: 93.1 us -> 30.4 us (0.33)
  the two profiles are of different devices: /device:TPU:1 before, /device:TPU:0 now
where the time goes in v1:
time: 30.4 us; the launch traced here: 30 us
  Pallas kernels  22 us (72%)
  local copies, waits for them, and re-layouts  7.33 us (24%)
  between operations  0.64 us (2%)
    pallas_call x1, Pallas kernels, body(): pl.pallas_call(functools.partial(kernel, nx, ny), out_shape=(jax.ShapeDty...  22 us
    unnamed x15, local copies, waits for them, and re-layouts  7.33 us

profile of v1, /device:TPU:0, one launch (start us, length us, event | category | flops | bytes accessed | tf_op | source)
XLA Modules:
  0.0 30.0 jit_solution(18003856837429932053)
XLA Ops:
  0.6 0.8 %copy.9.moduli = f32[8,3]{1,0:T(8,128)S(1)} copy(f32[8,3]{0,1:T(4,128)} %param.12) | data formatting | bytes 192 | tf_op args[5]
  1.4 0.0 copy-start
  1.4 1.4 %copy-done = f32[8,6,8,8,128]{4,3,2,1,0:T(8,128)S(1)} copy-done((f32[8,6,8,8,128]{4,3,2,1,0:T(8,128)S(1)}, f32[8,6,8,8,128]{4,3,2,1,0:T(8,128)}, u32[]{:S(2)}) %copy-start) | copy-done | bytes 1572888
  2.8 0.0 copy-start.1
  2.8 0.9 %copy-done.1 = f32[3,8,8,128]{3,2,1,0:T(8,128)S(1)} copy-done((f32[3,8,8,128]{3,2,1,0:T(8,128)S(1)}, f32[3,8,8,128]{3,2,1,0:T(8,128)}, u32[]{:S(2)}) %copy-start.1) | copy-done | bytes 98328
  3.7 0.0 copy-start.2
  3.7 0.8 %copy-done.2 = f32[8,8,128]{2,1,0:T(8,128)S(1)} copy-done((f32[8,8,128]{2,1,0:T(8,128)S(1)}, f32[8,8,128]{2,1,0:T(8,128)}, u32[]{:S(2)}) %copy-start.2) | copy-done | bytes 32792
  4.4 0.0 copy-start.3
  4.4 0.8 %copy-done.3 = s32[8,8,128]{2,1,0:T(8,128)S(1)} copy-done((s32[8,8,128]{2,1,0:T(8,128)S(1)}, s32[8,8,128]{2,1,0:T(8,128)}, u32[]{:S(2)}) %copy-start.3) | copy-done | bytes 32792
  5.2 0.0 copy-start.4
  5.2 0.8 %copy-done.4 = s32[8,8,128]{2,1,0:T(8,128)S(1)} copy-done((s32[8,8,128]{2,1,0:T(8,128)S(1)}, s32[8,8,128]{2,1,0:T(8,128)}, u32[]{:S(2)}) %copy-start.4) | copy-done | bytes 32792
  6.0 0.0 copy-start.5
  6.0 0.7 %copy-done.5 = f32[8,8]{1,0:T(8,128)S(1)} copy-done((f32[8,8]{1,0:T(8,128)S(1)}, f32[8,8]{1,0:T(8,128)}, u32[]{:S(2)}) %copy-start.5) | copy-done | bytes 280
  6.7 22.0 %shard_map.86 = (f32[3,8,8,128]{3,2,1,0:T(8,128)S(1)}, f32[6,8,8,128]{3,2,1,0:T(8,128)S(1)}) custom-call(f32[3,8,8,128]{3,2,1,0:T(8,128)S(1)} %copy-done.1, f32[8,6,8,8,128]{4,3,2,1,0:T(8,128)S(1)} %copy-done, f32[8,8,128]{2,1,0:T(8,128)S(1)} %copy-done.2, s32[8,8,128]{2,1,0:T(8,128)S(1)} %copy-done.3, s32[8,8,128]{2,1,0:T(8,128)S(1)} %copy-done.4, ...), custom_call_target="tpu_custom_call" | custom-call | tf_op jit(solution)/shard_map/pallas_call | solution.py:397
  28.7 0.6 %copy.12 = f32[3,8,8,128]{3,2,1,0:T(8,128)} copy(f32[3,8,8,128]{3,2,1,0:T(8,128)S(1)} %get-tuple-element.4) | data formatting | bytes 196608
  29.3 0.7 %copy.13 = f32[6,8,8,128]{3,2,1,0:T(8,128)} copy(f32[6,8,8,128]{3,2,1,0:T(8,128)S(1)} %get-tuple-element.5) | data formatting | bytes 393216
Async XLA Ops:
  1.4 1.4 %copy-start = (f32[8,6,8,8,128]{4,3,2,1,0:T(8,128)S(1)}, f32[8,6,8,8,128]{4,3,2,1,0:T(8,128)}, u32[]{:S(2)}) copy-start(f32[8,6,8,8,128]{4,3,2,1,0:T(8,128)} %surfaces.1) | copy-start | bytes 4718596
  2.8 0.9 %copy-start.1 = (f32[3,8,8,128]{3,2,1,0:T(8,128)S(1)}, f32[3,8,8,128]{3,2,1,0:T(8,128)}, u32[]{:S(2)}) copy-start(f32[3,8,8,128]{3,2,1,0:T(8,128)} %velocity.1) | copy-start | bytes 294916
  3.7 0.8 %copy-start.2 = (f32[8,8,128]{2,1,0:T(8,128)S(1)}, f32[8,8,128]{2,1,0:T(8,128)}, u32[]{:S(2)}) copy-start(f32[8,8,128]{2,1,0:T(8,128)} %mean_in.1) | copy-start | bytes 98308
  4.4 0.8 %copy-start.3 = (s32[8,8,128]{2,1,0:T(8,128)S(1)}, s32[8,8,128]{2,1,0:T(8,128)}, u32[]{:S(2)}) copy-start(s32[8,8,128]{2,1,0:T(8,128)} %zone.1) | copy-start | bytes 98308
  5.2 0.8 %copy-start.4 = (s32[8,8,128]{2,1,0:T(8,128)S(1)}, s32[8,8,128]{2,1,0:T(8,128)}, u32[]{:S(2)}) copy-start(s32[8,8,128]{2,1,0:T(8,128)} %sponge.1) | copy-start | bytes 98308
  6.0 0.7 %copy-start.5 = (f32[8,8]{1,0:T(8,128)S(1)}, f32[8,8]{1,0:T(8,128)}, u32[]{:S(2)}) copy-start(f32[8,8]{1,0:T(8,128)} %yields.1) | copy-start | bytes 772

commit v2 on v1

--- a/solution.py
+++ b/solution.py
@@ -30,17 +30,29 @@
 
 def kernel(
     nx, ny,
-    velocity, surfaces, mean_in, zone, sponge, moduli, yields,
+    velocity_hbm, surfaces, mean_hbm, zone_hbm, sponge_hbm, moduli_hbm, yields_hbm,
     velocity_out, stress_out,
-    surf, mean, S, V, A, D, bulk, shear, limit, strips,
+    velocity, zone, sponge, moduli, yields, surf, mean, S, V, A, D, bulk, shear, limit, strips,
     face_out, face_in, corner_out, corner_in,
     load_sem, face_send, face_recv, corner_send, corner_recv,
 ):
     px, py = lax.axis_index("gx"), lax.axis_index("gy")
     f32 = jnp.float32
 
-    load_surf = pltpu.make_async_copy(surfaces, surf, load_sem.at[0])
-    load_surf.start()
+    small = (
+        (moduli_hbm, moduli), (yields_hbm, yields), (zone_hbm, zone),
+        (sponge_hbm, sponge), (mean_hbm, mean), (velocity_hbm, velocity),
+    )
+    loads = [
+        pltpu.make_async_copy(source, target, load_sem.at[index])
+        for index, (source, target) in enumerate(small)
+    ]
+    surface_loads = [
+        pltpu.make_async_copy(surfaces.at[k], surf.at[k], load_sem.at[len(small) + k])
+        for k in range(SURF)
+    ]
+    for load in loads + surface_loads:
+        load.start()
 
     def has(axis, side):
         at, count = ((px, nx), (py, ny))[axis]
@@ -89,8 +101,14 @@
         strips[i, 0:8, :] = zero
         strips[i, 8:16, :] = zero
 
+    for load in loads:
+        load.wait()
+
+    modulus = lambda z, column: moduli[column, z]
+    strength = lambda z, column: yields[z, column]
+
     def pick(table, column, b0, b1, b2):
-        v = [table[z, column] for z in range(ZONES)]
+        v = [table(z, column) for z in range(ZONES)]
         a = [jnp.where(b0, v[2 * n + 1], v[2 * n]) for n in range(4)]
         c = [jnp.where(b1, a[2 * n + 1], a[2 * n]) for n in range(2)]
         return jnp.where(b2, c[1], c[0])
@@ -100,13 +118,12 @@
         z = zone[i]
         b0, b1, b2 = (z & 1) > 0, (z & 2) > 0, (z & 4) > 0
         damping = 1.0 - SPONGE * sponge[i].astype(f32)
-        bulk[i] = DT * pick(moduli, 0, b0, b1, b2)
-        shear[i] = (2.0 * DT / SURF) * pick(moduli, 1, b0, b1, b2)
-        A[i] = DT * pick(moduli, 2, b0, b1, b2) * damping
+        bulk[i] = DT * pick(modulus, 0, b0, b1, b2)
+        shear[i] = (2.0 * DT / SURF) * pick(modulus, 1, b0, b1, b2)
+        A[i] = DT * pick(modulus, 2, b0, b1, b2) * damping
         D[i] = damping
         for k in range(SURF):
-            limit[k, i] = pick(yields, k, b0, b1, b2)
-        mean[i] = mean_in[i]
+            limit[k, i] = pick(strength, k, b0, b1, b2)
         for c in range(3):
             V[c * WX + 2 + i, 4:12, :] = velocity[c, i]
 
@@ -171,15 +188,17 @@
     def get_a(axis, k):
         return A[k] if axis == 0 else A_rows[pl.ds(k, B, stride=B), :]
 
-    def face_copy(t, axis, side, toward):
+    def face_copy(t, axis, side, toward, part):
         own, other = (side + 1) // 2, (1 - side) // 2
-        tiles = pl.ds(0, 11 if t == 0 else 9)
+        split = 7 if side > 0 else 6
+        start, stop = (2 if t else 0, split) if part == 0 else (split, 11)
+        tiles = pl.ds(start, stop - start)
         shift = (toward, 0) if axis == 0 else (0, toward)
         return pltpu.make_async_remote_copy(
             src_ref=face_out.at[t, axis, own, tiles],
             dst_ref=face_in.at[t, axis, other, tiles],
-            send_sem=face_send.at[t, axis, own],
-            recv_sem=face_recv.at[t, axis, other],
+            send_sem=face_send.at[t, axis, own, part],
+            recv_sem=face_recv.at[t, axis, other, part],
             device_id=device(*shift),
             device_id_type=pl.DeviceIdType.MESH,
         )
@@ -213,32 +232,36 @@
             def _():
                 corner_copy(t, index, index).start()
 
-    def send_faces(t):
-        for axis, side in FACES:
-            n, tg, z = NORMAL[axis]
-            vn, vt, vz = VELOCITY[axis]
-            s = functools.partial(get_s, axis)
-            v = functools.partial(get_v, axis)
+    def send_face(t, axis, side, part):
+        n, tg, z = NORMAL[axis]
+        vn, vt, vz = VELOCITY[axis]
+        s = functools.partial(get_s, axis)
+        v = functools.partial(get_v, axis)
+        if part == 0:
             if side > 0:
-                tiles = [s(n, 7), s(tg, 6), s(tg, 7), s(z, 6), s(z, 7),
-                         v(vn, 6), v(vn, 7), v(vt, 7), v(vz, 7)]
-                a_from = 6
+                tiles = [s(n, 7), s(tg, 6), s(tg, 7), s(z, 6), s(z, 7)]
             else:
-                tiles = [s(n, 0), s(n, 1), s(tg, 0), s(z, 0),
-                         v(vn, 0), v(vt, 0), v(vt, 1), v(vz, 0), v(vz, 1)]
-                a_from = 0
+                tiles = [s(n, 0), s(n, 1), s(tg, 0), s(z, 0)]
+            start = 2
             if t == 0:
-                tiles += [get_a(axis, a_from), get_a(axis, a_from + 1)]
-            for index, tile in enumerate(tiles):
-                face_out[t, axis, (side + 1) // 2, index] = tile
-
-            @pl.when(has(axis, side))
-            def _():
-                face_copy(t, axis, side, side).start()
-
-    def partial_velocity():
-        @pl.loop(0, B)
-        def _(i):
+                start = 0
+                k = 6 if side > 0 else 0
+                tiles = [get_a(axis, k), get_a(axis, k + 1)] + tiles
+        elif side > 0:
+            tiles = [v(vn, 6), v(vn, 7), v(vt, 7), v(vz, 7)]
+            start = 7
+        else:
+            tiles = [v(vn, 0), v(vt, 0), v(vt, 1), v(vz, 0), v(vz, 1)]
+            start = 6
+        for index, tile in enumerate(tiles):
+            face_out[t, axis, (side + 1) // 2, start + index] = tile
+
+        @pl.when(has(axis, side))
+        def _():
+            face_copy(t, axis, side, side, part).start()
+
+    def partial_velocity(layers):
+        for i in layers:
             sx = functools.partial(along_x, S)
             sy = functools.partial(along_y, S)
             here = lambda c: S[c * WX + 2 + i, 4:12, :]
@@ -256,7 +279,8 @@
         for axis, side in FACES:
             @pl.when(has(axis, side))
             def _():
-                face_copy(t, axis, -side, side).wait_recv()
+                for part in range(2):
+                    face_copy(t, axis, -side, side, part).wait_recv()
         for index, (dx, dy) in enumerate(CORNERS):
             @pl.when(has_corner(dx, dy))
             def _():
@@ -283,10 +307,10 @@
             def strip(side, m, k):
                 return along_rows(strips, (axis * 2 + side) * 6 + m * 2 + k)
 
-            lo = lambda m: face_in[t, axis, 0, m]
-            hi = lambda m: face_in[t, axis, 1, m]
-            a_lo = lambda k: face_in[0, axis, 0, 9 + k]
-            a_hi = lambda k: face_in[0, axis, 1, 9 + k]
+            lo = lambda m: face_in[t, axis, 0, 2 + m]
+            hi = lambda m: face_in[t, axis, 1, 2 + m]
+            a_lo = lambda k: face_in[0, axis, 0, k]
+            a_hi = lambda k: face_in[0, axis, 1, k]
 
             set_v(axis, vn, -2, lo(5) + a_lo(0) * (
                 C2 * s(n, 0) + backward_of(strip(0, 0, 0))))
@@ -315,9 +339,9 @@
                 add(c, 1, -C2 * lo(m + 1))
                 add(c, 7, C2 * hi(h))
 
-    def plastic():
-        @pl.loop(0, B)
-        def _(i):
+    def plastic(last):
+        @functools.partial(lax.fori_loop, 0, B, init_val=None, unroll=2)
+        def _(i, _carry):
             vx = functools.partial(along_x, V)
             vy = functools.partial(along_y, V)
             here = lambda c: V[c * WX + 2 + i, 4:12, :]
@@ -345,12 +369,18 @@
                 factor = lim * lax.rsqrt(jnp.maximum(size2, lim * lim))
                 for c in range(6):
                     new = trial[c] * factor
-                    surf[k, c, i] = new
+                    if not last:
+                        surf[k, c, i] = new
                     total[c] = new if k == 0 else total[c] + new
             for c in range(6):
-                S[c * WX + 2 + i, 4:12, :] = total[c] + pressure if c < 3 else total[c]
-
-    load_surf.wait()
+                value = total[c] + pressure if c < 3 else total[c]
+                if last:
+                    stress_out[c, i] = value
+                else:
+                    S[c * WX + 2 + i, 4:12, :] = value
+
+    for load in surface_loads:
+        load.wait()
 
     @pl.loop(0, B)
     def _(i):
@@ -365,24 +395,28 @@
 
     for t in range(ITERS):
         send_corners(t)
-        partial_velocity()
-        send_faces(t)
+        for axis, side in FACES:
+            send_face(t, axis, side, 0)
+        partial_velocity((0, 1, 6, 7))
+        send_face(t, 0, -1, 1)
+        send_face(t, 0, 1, 1)
+        partial_velocity((2, 3, 4, 5))
+        send_face(t, 1, -1, 1)
+        send_face(t, 1, 1, 1)
         receive(t)
         finish_velocity(t)
-        plastic()
+        plastic(t == ITERS - 1)
 
     for c in range(3):
         for i in range(B):
             velocity_out[c, i] = V[c * WX + 2 + i, 4:12, :]
-    for c in range(6):
-        for i in range(B):
-            stress_out[c, i] = S[c * WX + 2 + i, 4:12, :]
 
     for t in range(ITERS):
         for axis, side in FACES:
             @pl.when(has(axis, side))
             def _():
-                face_copy(t, axis, side, side).wait_send()
+                for part in range(2):
+                    face_copy(t, axis, side, side, part).wait_send()
         for index, (dx, dy) in enumerate(CORNERS):
             @pl.when(has_corner(dx, dy))
             def _():
@@ -391,7 +425,6 @@
 
 def body(nx, ny, velocity, surfaces, mean_stress, zone, sponge, moduli, yields):
     vmem = pl.BlockSpec(memory_space=pltpu.VMEM)
-    smem = pl.BlockSpec(memory_space=pltpu.SMEM)
     f32 = jnp.float32
     tiles = lambda *lead: pltpu.VMEM(lead + (B, 128), f32)
     return pl.pallas_call(
@@ -400,9 +433,14 @@
             jax.ShapeDtypeStruct((3, B, B, 128), f32),
             jax.ShapeDtypeStruct((6, B, B, 128), f32),
         ),
-        in_specs=[vmem, pl.BlockSpec(memory_space=pl.ANY), vmem, vmem, vmem, smem, smem],
+        in_specs=[pl.BlockSpec(memory_space=pltpu.HBM)] * 7,
         out_specs=(vmem, vmem),
         scratch_shapes=[
+            tiles(3, B),
+            pltpu.VMEM((B, B, 128), jnp.int32),
+            pltpu.VMEM((B, B, 128), jnp.int32),
+            pltpu.SMEM((3, ZONES), f32),
+            pltpu.SMEM((ZONES, SURF), f32),
             tiles(SURF, 6, B),
             tiles(B),
             pltpu.VMEM((6 * WX, WY, 128), f32),
@@ -414,16 +452,19 @@
             tiles(ITERS, 2, 2, 11),
             pltpu.VMEM((ITERS, 4, 24, 128), f32),
             pltpu.VMEM((ITERS, 4, 24, 128), f32),
-            pltpu.SemaphoreType.DMA((1,)),
-            pltpu.SemaphoreType.DMA((ITERS, 2, 2)),
-            pltpu.SemaphoreType.DMA((ITERS, 2, 2)),
+            pltpu.SemaphoreType.DMA((6 + SURF,)),
+            pltpu.SemaphoreType.DMA((ITERS, 2, 2, 2)),
+            pltpu.SemaphoreType.DMA((ITERS, 2, 2, 2)),
             pltpu.SemaphoreType.DMA((ITERS, 4)),
             pltpu.SemaphoreType.DMA((ITERS, 4)),
         ],
         compiler_params=pltpu.CompilerParams(
             collective_id=0, has_side_effects=True, vmem_limit_bytes=32 << 20
         ),
-    )(velocity, surfaces, mean_stress, zone, sponge, moduli, yields)
+    )(*(
+        pltpu.with_memory_space_constraint(array, pltpu.HBM)
+        for array in (velocity, surfaces, mean_stress, zone, sponge, moduli.T, yields)
+    ))
 
 
 def solution(mesh):

time: 30.4 us -> 21.9 us (0.72)
  local copies, waits for them, and re-layouts: 7.33 us -> 1.32 us
  Pallas kernels: 22 us -> 19.7 us
    unnamed x15 -> x2, local copies, waits for them, and re-layouts: 7.33 us -> 1.32 us
    pallas_call x1, Pallas kernels: 22 us -> 19.7 us  [body(): pl.pallas_call(functools.partial(kernel, nx, ny), out_shape=(jax.ShapeDty...]
where the time goes in v2:
time: 21.9 us; the launch traced here: 21.7 us
  Pallas kernels  19.7 us (90%)
  local copies, waits for them, and re-layouts  1.32 us (6%)
  between operations  0.64 us (3%)
    pallas_call x1, Pallas kernels, body(): pl.pallas_call(functools.partial(kernel, nx, ny), out_shape=(jax.ShapeDty...  19.7 us
    unnamed x2, local copies, waits for them, and re-layouts  1.32 us

profile of v2, /device:TPU:0, one launch (start us, length us, event | category | flops | bytes accessed | tf_op | source)
XLA Modules:
  0.0 21.7 jit_solution(5967930499377431967)
XLA Ops:
  0.6 19.7 %shard_map.86 = (f32[3,8,8,128]{3,2,1,0:T(8,128)S(1)}, f32[6,8,8,128]{3,2,1,0:T(8,128)S(1)}) custom-call(f32[3,8,8,128]{3,2,1,0:T(8,128)} %velocity_hbm.1, f32[8,6,8,8,128]{4,3,2,1,0:T(8,128)} %surfaces.1, f32[8,8,128]{2,1,0:T(8,128)} %mean_hbm.1, s32[8,8,128]{2,1,0:T(8,128)} %zone_hbm.1, s32[8,8,128]{2,1,0:T(8,128)} %sponge_hbm.1, f32[3,8]{1,0:T(4,128)} %bitcast.1, ...), custom_call_target="tpu_custom_call" | custom-call | tf_op jit(solution)/shard_map/pallas_call | solution.py:430
  20.4 0.6 %copy.11 = f32[3,8,8,128]{3,2,1,0:T(8,128)} copy(f32[3,8,8,128]{3,2,1,0:T(8,128)S(1)} %get-tuple-element.4) | data formatting | bytes 196608
  21.0 0.7 %copy.12 = f32[6,8,8,128]{3,2,1,0:T(8,128)} copy(f32[6,8,8,128]{3,2,1,0:T(8,128)S(1)} %get-tuple-element.5) | data formatting | bytes 393216

commit v3 on v2

--- a/solution.py
+++ b/solution.py
@@ -26,6 +26,21 @@
 
 FACES = ((0, -1), (0, 1), (1, -1), (1, 1))
 CORNERS = ((-1, -1), (-1, 1), (1, -1), (1, 1))
+CORNER_ROWS = 16
+
+
+def corner_cells(ex, ey):
+    cells = set()
+    for axis, side, other in ((0, ex, ey), (1, ey, ex)):
+        for n, layers in enumerate(((0, 1), (1,), (1,)) if side < 0 else ((0,), (0, 1), (0, 1))):
+            if n == 1:
+                rows = (1,) if other < 0 else (0, 1)
+            else:
+                rows = (0, 1) if other < 0 else (0,)
+            for k in layers:
+                for r in rows:
+                    cells.add((ALONG[axis][n],) + ((k, r) if axis == 0 else (r, k)))
+    return sorted(cells)
 
 
 def kernel(
@@ -51,7 +66,7 @@
         pltpu.make_async_copy(surfaces.at[k], surf.at[k], load_sem.at[len(small) + k])
         for k in range(SURF)
     ]
-    for load in loads + surface_loads:
+    for load in surface_loads + loads:
         load.start()
 
     def has(axis, side):
@@ -88,8 +103,8 @@
         @pl.when(jnp.logical_not(has_corner(dx, dy)))
         def _():
             for t in range(ITERS):
-                for part in range(3):
-                    corner_in[t, index, part * 8:part * 8 + 8, :] = zero
+                corner_in[t, index, 0:8, :] = zero
+                corner_in[t, index, 8:16, :] = zero
 
     @pl.loop(0, 6 * WX)
     def _(i):
@@ -100,9 +115,6 @@
     def _(i):
         strips[i, 0:8, :] = zero
         strips[i, 8:16, :] = zero
-
-    for load in loads:
-        load.wait()
 
     modulus = lambda z, column: moduli[column, z]
     strength = lambda z, column: yields[z, column]
@@ -113,19 +125,26 @@
         c = [jnp.where(b1, a[2 * n + 1], a[2 * n]) for n in range(2)]
         return jnp.where(b2, c[1], c[0])
 
-    @pl.loop(0, B)
-    def _(i):
+    def zone_bits(i):
         z = zone[i]
-        b0, b1, b2 = (z & 1) > 0, (z & 2) > 0, (z & 4) > 0
-        damping = 1.0 - SPONGE * sponge[i].astype(f32)
-        bulk[i] = DT * pick(modulus, 0, b0, b1, b2)
-        shear[i] = (2.0 * DT / SURF) * pick(modulus, 1, b0, b1, b2)
-        A[i] = DT * pick(modulus, 2, b0, b1, b2) * damping
-        D[i] = damping
-        for k in range(SURF):
-            limit[k, i] = pick(strength, k, b0, b1, b2)
-        for c in range(3):
-            V[c * WX + 2 + i, 4:12, :] = velocity[c, i]
+        return (z & 1) > 0, (z & 2) > 0, (z & 4) > 0
+
+    def motion_factors():
+        for i in range(B):
+            damping = 1.0 - SPONGE * sponge[i].astype(f32)
+            A[i] = DT * pick(modulus, 2, *zone_bits(i)) * damping
+            D[i] = damping
+            for c in range(3):
+                V[c * WX + 2 + i, 4:12, :] = velocity[c, i]
+
+    def yield_factors():
+        @pl.loop(0, B)
+        def _(i):
+            bits = zone_bits(i)
+            bulk[i] = DT * pick(modulus, 0, *bits)
+            shear[i] = (2.0 * DT / SURF) * pick(modulus, 1, *bits)
+            for k in range(SURF):
+                limit[k, i] = pick(strength, k, *bits)
 
     lane = lax.broadcasted_iota(jnp.int32, (B, 128), 1)
 
@@ -190,8 +209,8 @@
 
     def face_copy(t, axis, side, toward, part):
         own, other = (side + 1) // 2, (1 - side) // 2
-        split = 7 if side > 0 else 6
-        start, stop = (2 if t else 0, split) if part == 0 else (split, 11)
+        split = 5 if side > 0 else 4
+        start, stop = (0, split) if part == 0 else (split, 9 if t else 11)
         tiles = pl.ds(start, stop - start)
         shift = (toward, 0) if axis == 0 else (0, toward)
         return pltpu.make_async_remote_copy(
@@ -205,9 +224,10 @@
 
     def corner_copy(t, index, toward):
         dx, dy = CORNERS[toward]
+        rows = pl.ds(0, len(corner_cells(*CORNERS[3 - index])))
         return pltpu.make_async_remote_copy(
-            src_ref=corner_out.at[t, index],
-            dst_ref=corner_in.at[t, 3 - index],
+            src_ref=corner_out.at[t, index, rows],
+            dst_ref=corner_in.at[t, 3 - index, rows],
             send_sem=corner_send.at[t, index],
             recv_sem=corner_recv.at[t, 3 - index],
             device_id=device(dx, dy),
@@ -217,16 +237,11 @@
     def send_corners(t):
         for index, (dx, dy) in enumerate(CORNERS):
             kx, ky = (6 if dx > 0 else 0), (6 if dy > 0 else 0)
-            for n in range(3):
-                for k in range(2):
-                    row = (n * 2 + k) * 2
-                    corner_out[t, index, row:row + 2, :] = S[
-                        ALONG[0][n] * WX + 2 + kx + k, 4 + ky:6 + ky, :
-                    ]
-                    for m in range(2):
-                        corner_out[t, index, 12 + row + m:13 + row + m, :] = S[
-                            ALONG[1][n] * WX + 2 + kx + m, 4 + ky + k:5 + ky + k, :
-                        ]
+            for row, (c, x, y) in enumerate(corner_cells(-dx, -dy)):
+                y_row = 4 + ky + y
+                corner_out[t, index, row:row + 1, :] = S[
+                    c * WX + 2 + kx + x, y_row:y_row + 1, :
+                ]
 
             @pl.when(has_corner(dx, dy))
             def _():
@@ -242,17 +257,16 @@
                 tiles = [s(n, 7), s(tg, 6), s(tg, 7), s(z, 6), s(z, 7)]
             else:
                 tiles = [s(n, 0), s(n, 1), s(tg, 0), s(z, 0)]
-            start = 2
-            if t == 0:
-                start = 0
-                k = 6 if side > 0 else 0
-                tiles = [get_a(axis, k), get_a(axis, k + 1)] + tiles
+            start = 0
         elif side > 0:
             tiles = [v(vn, 6), v(vn, 7), v(vt, 7), v(vz, 7)]
-            start = 7
+            start = 5
         else:
             tiles = [v(vn, 0), v(vt, 0), v(vt, 1), v(vz, 0), v(vz, 1)]
-            start = 6
+            start = 4
+        if part == 1 and t == 0:
+            k = 6 if side > 0 else 0
+            tiles += [get_a(axis, k), get_a(axis, k + 1)]
         for index, tile in enumerate(tiles):
             face_out[t, axis, (side + 1) // 2, start + index] = tile
 
@@ -275,73 +289,81 @@
                     D[i] * V[c * WX + 2 + i, 4:12, :] + A[i] * accel[c]
                 )
 
-    def receive(t):
-        for axis, side in FACES:
+    def receive_faces(t, axis):
+        for side in (-1, 1):
             @pl.when(has(axis, side))
             def _():
                 for part in range(2):
                     face_copy(t, axis, -side, side, part).wait_recv()
+
+    def receive_corners(t):
         for index, (dx, dy) in enumerate(CORNERS):
             @pl.when(has_corner(dx, dy))
             def _():
                 corner_copy(t, 3 - index, index).wait_recv()
 
-    def finish_velocity(t):
+    def finish_corners(t):
         for index, (dx, dy) in enumerate(CORNERS):
-            for axis, side, other in ((0, dx, dy), (1, dy, dx)):
-                at = 2 if other < 0 else 12
-                for n in range(6):
-                    row = axis * 12 + n * 2
-                    strips[(axis * 2 + (side + 1) // 2) * 6 + n, at:at + 2, :] = (
-                        corner_in[t, index, row:row + 2, :]
-                    )
+            for row, (c, x, y) in enumerate(corner_cells(dx, dy)):
+                cell = corner_in[t, index, row:row + 1, :]
+                for axis, side, other, k, r in ((0, dx, dy, x, y), (1, dy, dx, y, x)):
+                    if c in ALONG[axis]:
+                        strip = (axis * 2 + (side + 1) // 2) * 6 + ALONG[axis].index(c) * 2 + k
+                        at = (2 if other < 0 else 12) + r
+                        strips[strip, at:at + 1, :] = cell
         for axis in range(2):
-            n, tg, z = NORMAL[axis]
             vn, vt, vz = VELOCITY[axis]
-            s = functools.partial(get_s, axis)
-            a = functools.partial(get_a, axis)
-
-            def add(c, k, value):
-                set_v(axis, c, k, get_v(axis, c, k) + a(k) * value)
-
-            def strip(side, m, k):
-                return along_rows(strips, (axis * 2 + side) * 6 + m * 2 + k)
-
-            lo = lambda m: face_in[t, axis, 0, 2 + m]
-            hi = lambda m: face_in[t, axis, 1, 2 + m]
-            a_lo = lambda k: face_in[0, axis, 0, k]
-            a_hi = lambda k: face_in[0, axis, 1, k]
-
-            set_v(axis, vn, -2, lo(5) + a_lo(0) * (
-                C2 * s(n, 0) + backward_of(strip(0, 0, 0))))
-            set_v(axis, vn, -1, lo(6) + a_lo(1) * (
-                C1 * s(n, 0) + C2 * s(n, 1) + backward_of(strip(0, 0, 1))))
-            set_v(axis, vt, -1, lo(7) + a_lo(1) * (
-                C2 * s(tg, 0) + forward_of(strip(0, 1, 1))))
-            set_v(axis, vz, -1, lo(8) + a_lo(1) * (
-                C2 * s(z, 0) + backward_of(strip(0, 2, 1))))
-            set_v(axis, vn, 8, hi(4) + a_hi(0) * (
-                -C2 * s(n, 7) + backward_of(strip(1, 0, 0))))
-            set_v(axis, vt, 8, hi(5) + a_hi(0) * (
-                -C1 * s(tg, 7) - C2 * s(tg, 6) + forward_of(strip(1, 1, 0))))
-            set_v(axis, vt, 9, hi(6) + a_hi(1) * (
-                -C2 * s(tg, 7) + forward_of(strip(1, 1, 1))))
-            set_v(axis, vz, 8, hi(7) + a_hi(0) * (
-                -C1 * s(z, 7) - C2 * s(z, 6) + backward_of(strip(1, 2, 0))))
-            set_v(axis, vz, 9, hi(8) + a_hi(1) * (
-                -C2 * s(z, 7) + backward_of(strip(1, 2, 1))))
-
-            add(vn, 0, -C2 * lo(0))
-            add(vn, 6, C2 * hi(0))
-            add(vn, 7, C1 * hi(0) + C2 * hi(1))
-            for c, m, h in ((vt, 1, 2), (vz, 3, 3)):
-                add(c, 0, -C1 * lo(m + 1) - C2 * lo(m))
-                add(c, 1, -C2 * lo(m + 1))
-                add(c, 7, C2 * hi(h))
-
-    def plastic(last):
-        @functools.partial(lax.fori_loop, 0, B, init_val=None, unroll=2)
-        def _(i, _carry):
+
+            def add(c, side, m, k, derivative):
+                at = -2 + k if side == 0 else 8 + k
+                strip = along_rows(strips, (axis * 2 + side) * 6 + m * 2 + k)
+                factor = face_in[0, axis, side, 9 + k]
+                set_v(axis, c, at, get_v(axis, c, at) + factor * derivative(strip))
+
+            add(vn, 0, 0, 0, backward_of)
+            add(vn, 0, 0, 1, backward_of)
+            add(vt, 0, 1, 1, forward_of)
+            add(vz, 0, 2, 1, backward_of)
+            add(vn, 1, 0, 0, backward_of)
+            add(vt, 1, 1, 0, forward_of)
+            add(vt, 1, 1, 1, forward_of)
+            add(vz, 1, 2, 0, backward_of)
+            add(vz, 1, 2, 1, backward_of)
+
+    def finish_faces(t, axis):
+        n, tg, z = NORMAL[axis]
+        vn, vt, vz = VELOCITY[axis]
+        s = functools.partial(get_s, axis)
+        a = functools.partial(get_a, axis)
+
+        def add(c, k, value):
+            set_v(axis, c, k, get_v(axis, c, k) + a(k) * value)
+
+        lo = lambda m: face_in[t, axis, 0, m]
+        hi = lambda m: face_in[t, axis, 1, m]
+        a_lo = lambda k: face_in[0, axis, 0, 9 + k]
+        a_hi = lambda k: face_in[0, axis, 1, 9 + k]
+
+        set_v(axis, vn, -2, lo(5) + a_lo(0) * (C2 * s(n, 0)))
+        set_v(axis, vn, -1, lo(6) + a_lo(1) * (C1 * s(n, 0) + C2 * s(n, 1)))
+        set_v(axis, vt, -1, lo(7) + a_lo(1) * (C2 * s(tg, 0)))
+        set_v(axis, vz, -1, lo(8) + a_lo(1) * (C2 * s(z, 0)))
+        set_v(axis, vn, 8, hi(4) + a_hi(0) * (-C2 * s(n, 7)))
+        set_v(axis, vt, 8, hi(5) + a_hi(0) * (-C1 * s(tg, 7) - C2 * s(tg, 6)))
+        set_v(axis, vt, 9, hi(6) + a_hi(1) * (-C2 * s(tg, 7)))
+        set_v(axis, vz, 8, hi(7) + a_hi(0) * (-C1 * s(z, 7) - C2 * s(z, 6)))
+        set_v(axis, vz, 9, hi(8) + a_hi(1) * (-C2 * s(z, 7)))
+
+        add(vn, 0, -C2 * lo(0))
+        add(vn, 6, C2 * hi(0))
+        add(vn, 7, C1 * hi(0) + C2 * hi(1))
+        for c, m, h in ((vt, 1, 2), (vz, 3, 3)):
+            add(c, 0, -C1 * lo(m + 1) - C2 * lo(m))
+            add(c, 1, -C2 * lo(m + 1))
+            add(c, 7, C2 * hi(h))
+
+    def plastic(last, layers):
+        for i in layers:
             vx = functools.partial(along_x, V)
             vy = functools.partial(along_y, V)
             here = lambda c: V[c * WX + 2 + i, 4:12, :]
@@ -378,12 +400,15 @@
                     stress_out[c, i] = value
                 else:
                     S[c * WX + 2 + i, 4:12, :] = value
-
-    for load in surface_loads:
+            if last:
+                for c in range(3):
+                    velocity_out[c, i] = here(c)
+
+    for load in surface_loads + loads:
         load.wait()
 
-    @pl.loop(0, B)
-    def _(i):
+    @functools.partial(lax.fori_loop, 0, B, init_val=None, unroll=2)
+    def _(i, _carry):
         for c in range(6):
             total = surf[0, c, i]
             for k in range(1, SURF):
@@ -397,19 +422,28 @@
         send_corners(t)
         for axis, side in FACES:
             send_face(t, axis, side, 0)
+        if t == 0:
+            motion_factors()
         partial_velocity((0, 1, 6, 7))
         send_face(t, 0, -1, 1)
         send_face(t, 0, 1, 1)
         partial_velocity((2, 3, 4, 5))
         send_face(t, 1, -1, 1)
         send_face(t, 1, 1, 1)
-        receive(t)
-        finish_velocity(t)
-        plastic(t == ITERS - 1)
-
-    for c in range(3):
-        for i in range(B):
-            velocity_out[c, i] = V[c * WX + 2 + i, 4:12, :]
+        if t == 0:
+            yield_factors()
+        last = t == ITERS - 1
+        receive_faces(t, 1)
+        finish_faces(t, 1)
+        plastic(last, (3, 4))
+        receive_faces(t, 0)
+        finish_faces(t, 0)
+        receive_corners(t)
+        finish_corners(t)
+
+        @pl.loop(0, 3)
+        def _(j):
+            plastic(last, (j, j + 5))
 
     for t in range(ITERS):
         for axis, side in FACES:
@@ -450,8 +484,8 @@
             pltpu.VMEM((24, WY, 128), f32),
             tiles(ITERS, 2, 2, 11),
             tiles(ITERS, 2, 2, 11),
-            pltpu.VMEM((ITERS, 4, 24, 128), f32),
-            pltpu.VMEM((ITERS, 4, 24, 128), f32),
+            pltpu.VMEM((ITERS, 4, CORNER_ROWS, 128), f32),
+            pltpu.VMEM((ITERS, 4, CORNER_ROWS, 128), f32),
             pltpu.SemaphoreType.DMA((6 + SURF,)),
             pltpu.SemaphoreType.DMA((ITERS, 2, 2, 2)),
             pltpu.SemaphoreType.DMA((ITERS, 2, 2, 2)),

time: 21.9 us -> 20.3 us (0.927)
  Pallas kernels: 19.7 us -> 18.2 us
    pallas_call x1, Pallas kernels: 19.7 us -> 18.2 us  [body(): pl.pallas_call(functools.partial(kernel, nx, ny), out_shape=(jax.ShapeDty...]
where the time goes in v3:
time: 20.3 us; the launch traced here: 20.2 us
  Pallas kernels  18.2 us (90%)
  local copies, waits for them, and re-layouts  1.32 us (7%)
  between operations  0.64 us (3%)
    pallas_call x1, Pallas kernels, body(): pl.pallas_call(functools.partial(kernel, nx, ny), out_shape=(jax.ShapeDty...  18.2 us
    unnamed x2, local copies, waits for them, and re-layouts  1.32 us

profile of v3, /device:TPU:0, one launch (start us, length us, event | category | flops | bytes accessed | tf_op | source)
XLA Modules:
  0.0 20.2 jit_solution(3082299888476533899)
XLA Ops:
  0.6 18.2 %shard_map.86 = (f32[3,8,8,128]{3,2,1,0:T(8,128)S(1)}, f32[6,8,8,128]{3,2,1,0:T(8,128)S(1)}) custom-call(f32[3,8,8,128]{3,2,1,0:T(8,128)} %velocity_hbm.1, f32[8,6,8,8,128]{4,3,2,1,0:T(8,128)} %surfaces.1, f32[8,8,128]{2,1,0:T(8,128)} %mean_hbm.1, s32[8,8,128]{2,1,0:T(8,128)} %zone_hbm.1, s32[8,8,128]{2,1,0:T(8,128)} %sponge_hbm.1, f32[3,8]{1,0:T(4,128)} %bitcast.1, ...), custom_call_target="tpu_custom_call" | custom-call | tf_op jit(solution)/shard_map/pallas_call | solution.py:464
  18.8 0.6 %copy.11 = f32[3,8,8,128]{3,2,1,0:T(8,128)} copy(f32[3,8,8,128]{3,2,1,0:T(8,128)S(1)} %get-tuple-element.4) | data formatting | bytes 196608
  19.5 0.7 %copy.12 = f32[6,8,8,128]{3,2,1,0:T(8,128)} copy(f32[6,8,8,128]{3,2,1,0:T(8,128)S(1)} %get-tuple-element.5) | data formatting | bytes 393216

commit v4 on v3

--- a/solution.py
+++ b/solution.py
@@ -66,7 +66,7 @@
         pltpu.make_async_copy(surfaces.at[k], surf.at[k], load_sem.at[len(small) + k])
         for k in range(SURF)
     ]
-    for load in surface_loads + loads:
+    for load in loads + surface_loads:
         load.start()
 
     def has(axis, side):
@@ -404,7 +404,10 @@
                 for c in range(3):
                     velocity_out[c, i] = here(c)
 
-    for load in surface_loads + loads:
+    for load in loads:
+        load.wait()
+    motion_factors()
+    for load in surface_loads:
         load.wait()
 
     @functools.partial(lax.fori_loop, 0, B, init_val=None, unroll=2)
@@ -420,13 +423,13 @@
 
     for t in range(ITERS):
         send_corners(t)
-        for axis, side in FACES:
-            send_face(t, axis, side, 0)
-        if t == 0:
-            motion_factors()
+        send_face(t, 0, -1, 0)
+        send_face(t, 0, 1, 0)
         partial_velocity((0, 1, 6, 7))
         send_face(t, 0, -1, 1)
         send_face(t, 0, 1, 1)
+        send_face(t, 1, -1, 0)
+        send_face(t, 1, 1, 0)
         partial_velocity((2, 3, 4, 5))
         send_face(t, 1, -1, 1)
         send_face(t, 1, 1, 1)

time: 20.3 us -> 20.3 us (level)
  no operation moved by 1% of the time
where the time goes in v4:
time: 20.3 us; the launch traced here: 20.2 us
  Pallas kernels  18.2 us (90%)
  local copies, waits for them, and re-layouts  1.32 us (7%)
  between operations  0.64 us (3%)
    pallas_call x1, Pallas kernels, body(): pl.pallas_call(functools.partial(kernel, nx, ny), out_shape=(jax.ShapeDty...  18.2 us
    unnamed x2, local copies, waits for them, and re-layouts  1.32 us

profile of v4, /device:TPU:0, one launch (start us, length us, event | category | flops | bytes accessed | tf_op | source)
XLA Modules:
  0.0 20.2 jit_solution(485347573813280273)
XLA Ops:
  0.6 18.2 %shard_map.86 = (f32[3,8,8,128]{3,2,1,0:T(8,128)S(1)}, f32[6,8,8,128]{3,2,1,0:T(8,128)S(1)}) custom-call(f32[3,8,8,128]{3,2,1,0:T(8,128)} %velocity_hbm.1, f32[8,6,8,8,128]{4,3,2,1,0:T(8,128)} %surfaces.1, f32[8,8,128]{2,1,0:T(8,128)} %mean_hbm.1, s32[8,8,128]{2,1,0:T(8,128)} %zone_hbm.1, s32[8,8,128]{2,1,0:T(8,128)} %sponge_hbm.1, f32[3,8]{1,0:T(4,128)} %bitcast.1, ...), custom_call_target="tpu_custom_call" | custom-call | tf_op jit(solution)/shard_map/pallas_call | solution.py:467
  18.8 0.6 %copy.11 = f32[3,8,8,128]{3,2,1,0:T(8,128)} copy(f32[3,8,8,128]{3,2,1,0:T(8,128)S(1)} %get-tuple-element.4) | data formatting | bytes 196608
  19.5 0.7 %copy.12 = f32[6,8,8,128]{3,2,1,0:T(8,128)} copy(f32[6,8,8,128]{3,2,1,0:T(8,128)S(1)} %get-tuple-element.5) | data formatting | bytes 393216
